TPU v7x, 32 devices: a whole 2x2x4 slice. The times are simulated.
32 devices in a mesh: dp: 16 (over z, y, core), tensor: 2 (over x).
Axes of the slice: x: 2, y: 2, z: 4, core: 2. Of those that a mesh axis runs over, the one named last changes fastest.
Arguments:
- clip_feats: bfloat16 [2048, 1280], P('dp', 'tensor'), may hold values from -3 to 3
- proj_weight: bfloat16 [1280, 512], P('tensor'), may hold values from -1 to 1
- caption_emb: bfloat16 [2048, 512], P(('dp', 'tensor')), may hold values from -1.25 to 1.25
- logit_scale: float32 [1], replicated, may hold values from 20 to 400
- pair_perm: int32 [2048], replicated, may hold values from 0 to 2047, as said below
Outputs:
- clip_grad: float32 [2048, 1280], P('dp', 'tensor')
- caption_grad: float32 [2048, 512], P(('dp', 'tensor'))
- row_loss: float32 [2048], P('dp')
Inputs may be any that keep to these rules, and one draw needn't show every extreme that they name: pair_perm is a permutation of the 2048 caption indices.
All inputs are finite; a program needn't handle non-finite values.
Results may differ from a plain program's by a relative error of at most 0.012.
The roundings to bfloat16 on the way count: a program that leaves them out, or rounds other values in their place, can miss the bound.
Values may be sent and summed in bfloat16 or wider, within the bound.
A program may use at most 64 MiB of HBM per device.

v0:
```python
import jax
import jax.numpy as jnp
from jax import lax
from jax.sharding import PartitionSpec as P

norm_eps = 1e-06


def unit_rows(values):
    squares = jnp.sum(values * values, axis=1, keepdims=True)
    inverse = lax.rsqrt(squares + norm_eps)
    return (values * inverse, inverse)


def score_slab(videos, slab_rows, offset, target, logit):
    scores = logit * lax.dot_general(
        videos, slab_rows, (((1,), (1,)), ((), ())), preferred_element_type=jnp.float32
    )
    column = offset + jnp.arange(slab_rows.shape[0], dtype=jnp.int32)
    onehot = (column[None, :] == target[:, None]).astype(jnp.float32)
    return (scores, onehot)


def fold_stats(carry, slab_rows, offset, videos, target, logit):
    run_max, run_sum, run_pos = carry
    scores, onehot = score_slab(videos, slab_rows, offset, target, logit)
    new_max = jnp.maximum(run_max, jnp.max(scores, axis=1))
    run_sum = jnp.sum(jnp.exp(scores - new_max[:, None]), axis=1)
    run_pos = jnp.sum(scores * onehot, axis=1)
    return (new_max, run_sum, run_pos)


def slab_weights(slab_rows, offset, videos, target, logit, row_max, row_sum):
    scores, onehot = score_slab(videos, slab_rows, offset, target, logit)
    weights = (jnp.exp(scores - row_max[:, None]) / row_sum[:, None] - onehot).astype(jnp.bfloat16)
    vid_part = logit * jnp.dot(weights, slab_rows, preferred_element_type=jnp.float32)
    return (weights, vid_part)


def body(clip_feats, proj_weight, caption_emb, logit_scale, pair_perm):
    logit = logit_scale[0]
    partial_value = jnp.dot(clip_feats, proj_weight, preferred_element_type=jnp.float32)
    raw_proj = lax.psum(partial_value, "tensor")
    unit_vid, vid_inv = unit_rows(raw_proj)
    videos = unit_vid.astype(jnp.bfloat16)
    cap_unit, cap_inv = unit_rows(caption_emb.astype(jnp.float32))
    captions = cap_unit.astype(jnp.bfloat16)
    row_count = videos.shape[0]
    cap_count = captions.shape[0]
    groups = lax.axis_size("tensor")
    tensor_pos = lax.axis_index("tensor")
    wanted = lax.dynamic_slice_in_dim(pair_perm, lax.axis_index("dp") * row_count, row_count, 0)
    owner_block = wanted // cap_count
    local_col = owner_block // groups * cap_count + wanted % cap_count
    target = jnp.where(owner_block % groups == tensor_pos, local_col, -1)
    start_stats = (
        jnp.full((row_count,), -1e30, jnp.float32),
        jnp.zeros((row_count,), jnp.float32),
        jnp.zeros((row_count,), jnp.float32),
    )
    gathered = lax.all_gather(captions, "dp", axis=0, tiled=True)
    stats = fold_stats(start_stats, gathered, 0, videos, target, logit)
    row_max = lax.pmax(stats[0], "tensor")
    row_sum, row_pos = lax.psum((stats[1] * jnp.exp(stats[0] - row_max), stats[2]), "tensor")
    losses = row_max + jnp.log(row_sum) - row_pos
    weights_all, vid_part = slab_weights(gathered, 0, videos, target, logit, row_max, row_sum)
    vid_grad = lax.psum(vid_part, "tensor")
    cap_part = logit * lax.dot_general(
        weights_all, videos, (((0,), (0,)), ((), ())), preferred_element_type=jnp.float32
    )
    cap_grad = lax.psum_scatter(cap_part, "dp", scatter_dimension=0, tiled=True)
    vid_dot = jnp.sum(unit_vid * vid_grad, axis=1, keepdims=True)
    raw_grad = ((vid_grad - unit_vid * vid_dot) * vid_inv).astype(jnp.bfloat16)
    clip_grad = lax.dot_general(
        raw_grad, proj_weight, (((1,), (1,)), ((), ())), preferred_element_type=jnp.float32
    )
    cap_dot = jnp.sum(cap_unit * cap_grad, axis=1, keepdims=True)
    caption_grad = (cap_grad - cap_unit * cap_dot) * cap_inv
    return (clip_grad, caption_grad, losses)


def solution(mesh):
    return jax.shard_map(
        body,
        mesh=mesh,
        in_specs=(P("dp", "tensor"), P("tensor", None), P(("dp", "tensor"), None), P(), P()),
        out_specs=(P("dp", "tensor"), P(("dp", "tensor"), None), P("dp")),
        check_vma=False,
    )
```

profile of v0, /device:TPU:0, one launch (start us, length us, event | category | flops | bytes accessed | tf_op | source)
XLA Modules:
  0.0 143.4 jit_solution(11747821214149107070)
XLA Ops:
  8.0 0.0 copy-start
  8.0 0.0 all-reduce.4.cloned.1.call-start
  8.1 1.0 copy-done
  9.1 1.9 %fusion.12 = f32[128,512]{1,0:T(8,128)} fusion(bf16[128,640]{1,0:T(8,128)(2,1)} %param.5, bf16[640,512]{1,0:T(8,128)(2,1)S(1)} %copy-done), kind=kOutput, calls=%fused_computation.41 | convolution fusion | flops 83886080 | bytes 1081344 | tf_op jit(solution)/shard_map/dot_general | solution.py:42
  11.0 0.0 all-reduce.4.cloned.1.call-update
  11.0 0.0 all-gather.2.cloned.1.call-start
  11.1 1.0 fusion.6
  12.0 1.6 %fusion.2 = bf16[64,512]{1,0:T(8,128)(2,1)} fusion(bf16[64,512]{1,0:T(8,128)(2,1)} %param.7, f32[64]{0:T(128)S(1)} %add_rsqrt_fusion), kind=kLoop, calls=%fused_computation.15 | loop fusion | flops 98304 | bytes 131328 | tf_op jit(solution)/shard_map/convert_element_type | solution.py:47
  13.6 0.0 all-gather.2.cloned.1.call-update
  13.6 0.0 all-reduce.6.cloned.1.call-start
  14.3 0.8 compare_select_fusion
  15.1 22.6 %all-reduce.4.cloned.1.call-done = f32[128,512]{1,0:T(8,128)} async-done(((f32[128,512]{1,0:T(8,128)}), f32[128,512]{1,0:T(8,128)}) %all-reduce.4.cloned.1.call-update) | async-done | bytes 262160 | tf_op jit(solution)/shard_map/psum | solution.py:43
  37.7 1.1 multiply_reduce_fusion.1
  38.8 16.0 %all-gather.2.cloned.1.call-done = bf16[1024,512]{1,0:T(8,128)(2,1)} async-done(((bf16[64,512]{1,0:T(8,128)(2,1)}), bf16[1024,512]{1,0:T(8,128)(2,1)}) %all-gather.2.cloned.1.call-update) | async-done | bytes 1048592 | tf_op jit(solution)/shard_map/all_gather | solution.py:61
  54.8 0.0 copy-start.3
  54.8 1.9 %fusion.11 = (f32[128]{0:T(128)S(1)}, f32[128,1024]{1,0:T(8,128)S(1)}) fusion(bf16[1024,512]{1,0:T(8,128)(2,1)} %all-gather.2.cloned.1.call-done, f32[128,512]{1,0:T(8,128)} %all-reduce.4.cloned.1.call-done, f32[128]{0:T(128)S(1)} %add_rsqrt_fusion.1, f32[]{:T(128)} %bitcast.7), kind=kOutput, calls=%fused_computation.40 | convolution fusion | flops 134610816 | bytes 1836036 | tf_op jit(solution)/shard_map/dot_general | solution.py:16
  56.8 0.0 copy-start.1
  56.8 5.1 %pmax.7 = f32[128]{0:T(128)S(1)} all-reduce(f32[128]{0:T(128)S(1)} %broadcast_maximum_fusion), channel_id=1, replica_groups=mesh['dp'=16,'tensor'=2] {'tensor'}, use_global_device_ids=true, to_apply=%region_4.5 | all-reduce | flops 128 | bytes 1024 | tf_op jit(solution)/shard_map/pmax | solution.py:63
  61.9 0.3 select_reduce_fusion
  62.2 4.9 %all-reduce = (f32[128]{0:T(128)S(1)}, f32[128]{0:T(128)S(1)}) all-reduce(f32[128]{0:T(128)S(1)} %exponential_multiply_fusion, f32[128]{0:T(128)S(1)} %get-tuple-element.3), channel_id=1, replica_groups=mesh['dp'=16,'tensor'=2] {'tensor'}, use_global_device_ids=true, to_apply=%region_6.7 | all-reduce | flops 256 | bytes 2048 | tf_op jit(solution)/shard_map/psum | solution.py:64
  67.1 0.0 copy-done.3
  67.1 1.1 convolution_multiply_fusion.2
  68.2 0.0 all-reduce.6.cloned.1.call-update
  68.2 0.0 reduce-scatter.2.cloned.1.call-start
  68.3 0.0 copy-done.1
  68.3 2.0 %convolution_multiply_fusion = f32[1024,512]{1,0:T(8,128)} fusion(f32[]{:T(128)} %bitcast.8, f32[128,512]{1,0:T(8,128)S(1)} %copy-done.1, f32[128]{0:T(128)S(1)} %add_rsqrt_fusion.1, f32[128,1024]{1,0:T(8,128)S(1)} %get-tuple-element.8, s32[128]{0:T(128)S(1)} %compare_select_fusion, f32[128]{0:T(128)S(1)} %get-tuple-element.5, f32[128]{0:T(128)S(1)} %pmax.7), kind=kOutput, calls=%fused_computation | convolution fusion | flops 135659520 | bytes 2885636 | tf_op jit(solution)/shard_map/dot_general | solution.py:68
  70.2 0.0 copy-start.2
  70.2 0.0 reduce-scatter.2.cloned.1.call-update
  70.3 0.5 add_subtract_fusion
  70.8 19.9 %all-reduce.6.cloned.1.call-done = f32[128,512]{1,0:T(8,128)} async-done(((f32[128,512]{1,0:T(8,128)}), f32[128,512]{1,0:T(8,128)}) %all-reduce.6.cloned.1.call-update) | async-done | bytes 262160 | tf_op jit(solution)/shard_map/psum | solution.py:67
  90.7 1.1 multiply_reduce_fusion
  91.8 2.0 %fusion.7 = f32[128,640]{1,0:T(8,128)} fusion(bf16[640,512]{1,0:T(8,128)(2,1)S(1)} %copy-done, f32[128,512]{1,0:T(8,128)} %all-reduce.6.cloned.1.call-done, f32[128,512]{1,0:T(8,128)S(1)} %copy-done.1, f32[128]{0:T(128)S(1)} %multiply_reduce_fusion, f32[128]{0:T(128)S(1)} %add_rsqrt_fusion.1), kind=kOutput, calls=%fused_computation.20 | convolution fusion | flops 84213760 | bytes 1508352 | tf_op jit(solution)/shard_map/dot_general | solution.py:74
  93.9 39.4 %reduce-scatter.2.cloned.1.call-done = f32[64,512]{1,0:T(8,128)} async-done(((f32[1024,512]{1,0:T(8,128)}), f32[64,512]{1,0:T(8,128)}) %reduce-scatter.2.cloned.1.call-update) | async-done | bytes 131088 | tf_op jit(solution)/shard_map/reduce_scatter | solution.py:71
  133.3 0.0 copy-done.2
  133.3 1.1 fusion.3
  134.3 1.7 %fusion.5 = f32[64,512]{1,0:T(8,128)} fusion(f32[64,512]{1,0:T(8,128)} %reduce-scatter.2.cloned.1.call-done, bf16[64,512]{1,0:T(8,128)(2,1)S(1)} %copy-done.2, f32[64]{0:T(128)S(1)} %fusion.3, f32[64]{0:T(128)S(1)} %add_rsqrt_fusion), kind=kLoop, calls=%fused_computation.18 | loop fusion | flops 163840 | bytes 328192 | tf_op jit(solution)/shard_map/mul | solution.py:78
  (4 shorter events, 0.0 us)
Async XLA Ops:
  8.0 1.1 copy-start
  8.0 29.7 %all-reduce.4.cloned.1.call-start = ((), (), s32[]{:S(2)}) async-start(), calls=%async_computation.1 | async-start | bytes 524288 | tf_op jit(solution)/shard_map/psum | solution.py:43
  11.0 43.8 %all-gather.2.cloned.1.call-start = ((), (), s32[]{:S(2)}) async-start(), calls=%async_computation.2 | async-start | bytes 1114112 | tf_op jit(solution)/shard_map/all_gather | solution.py:61
  13.6 77.1 %all-reduce.6.cloned.1.call-start = ((), (), s32[]{:S(2)}) async-start(), calls=%async_computation.3 | async-start | bytes 524288 | tf_op jit(solution)/shard_map/psum | solution.py:67
  54.8 12.3 %copy-start.3 = (bf16[1024,512]{1,0:T(8,128)(2,1)S(1)}, bf16[1024,512]{1,0:T(8,128)(2,1)}, u32[]{:S(2)}) copy-start(bf16[1024,512]{1,0:T(8,128)(2,1)} %all-gather.2.cloned.1.call-done) | copy-start | bytes 3145732
  56.8 11.5 %copy-start.1 = (f32[128,512]{1,0:T(8,128)S(1)}, f32[128,512]{1,0:T(8,128)}, u32[]{:S(2)}) copy-start(f32[128,512]{1,0:T(8,128)} %all-reduce.4.cloned.1.call-done) | copy-start | bytes 786436
  68.2 65.0 %reduce-scatter.2.cloned.1.call-start = ((), (), s32[]{:S(2)}) async-start(), calls=%async_computation.4 | async-start | bytes 2228224 | tf_op jit(solution)/shard_map/reduce_scatter | solution.py:71
  70.2 63.0 %copy-start.2 = (bf16[64,512]{1,0:T(8,128)(2,1)S(1)}, bf16[64,512]{1,0:T(8,128)(2,1)}, u32[]{:S(2)}) copy-start(bf16[64,512]{1,0:T(8,128)(2,1)} %param.7) | copy-start | bytes 196612
Sparse Core Ops, SparseCore 0:
  11.7 26.0 all-reduce.3
  68.3 22.3 all-reduce.5
Sparse Core Ops, SparseCore 1:
  14.2 40.6 all-gather.1
  72.4 60.8 reduce-scatter.1
where the time goes:
time: 144 us; the launch traced here: 143 us
  waiting for transfers between devices  98 us (68%)
  between operations  16.2 us (11%)
  blocking collectives  10 us (7%)
  other arithmetic  9.03 us (6%)
  matrix products  8.93 us (6%)
    reduce_scatter x1, waiting for transfers between devices, body(): cap_grad = lax.psum_scatter(cap_part, 'dp', scatter_dimension=0, tiled=True)  39.4 us
    psum x1, waiting for transfers between devices, body(): raw_proj = lax.psum(partial_value, 'tensor')  22.6 us
    psum x1, waiting for transfers between devices, body(): vid_grad = lax.psum(vid_part, 'tensor')  19.9 us
    all_gather x1, waiting for transfers between devices, body(): gathered = lax.all_gather(captions, 'dp', axis=0, tiled=True)  16 us
    pmax x1, blocking collectives, body(): row_max = lax.pmax(stats[0], 'tensor')  5.07 us
    psum x1, blocking collectives, body(): lax.psum((stats[1] * jnp.exp(stats[0] - row_max), stats[2]), 'tensor')  4.93 us
  transfers between devices with their start and end apart: 4, of which 4 were waited for; matrix products, arithmetic and copies ran while one was open for 7% of the time, Pallas kernels for 0%

commit v1 on v0

--- a/solution.py
+++ b/solution.py
@@ -40,7 +40,7 @@
 def body(clip_feats, proj_weight, caption_emb, logit_scale, pair_perm):
     logit = logit_scale[0]
     partial_value = jnp.dot(clip_feats, proj_weight, preferred_element_type=jnp.float32)
-    raw_proj = lax.psum(partial_value, "tensor")
+    raw_proj = partial_value + lax.ppermute(partial_value, "tensor", [(0, 1), (1, 0)])
     unit_vid, vid_inv = unit_rows(raw_proj)
     videos = unit_vid.astype(jnp.bfloat16)
     cap_unit, cap_inv = unit_rows(caption_emb.astype(jnp.float32))

time: 144 us -> 162 us (1.12)
  waiting for transfers between devices: 98 us -> 118 us
  starting transfers between devices: 0.17 us -> 3.15 us
  between operations: 16.2 us -> 14.5 us
    reduce_scatter x1, waiting for transfers between devices: 39.4 us -> 62.4 us  [body(): cap_grad = lax.psum_scatter(cap_part, 'dp', scatter_dimension=0, tiled=True)]
    psum x1 -> x0, waiting for transfers between devices: 22.6 us -> none  [body(): raw_proj = lax.psum(partial_value, 'tensor')]
    all_gather x1, waiting for transfers between devices: 16 us -> 30.8 us  [body(): gathered = lax.all_gather(captions, 'dp', axis=0, tiled=True)]
    ppermute x0 -> x1, waiting for transfers between devices: none -> 4.87 us  [body(): lax.ppermute(partial_value, 'tensor', [(0, 1), (1, 0)])]
    ppermute x0 -> x1, starting transfers between devices: none -> 3.03 us  [body(): lax.ppermute(partial_value, 'tensor', [(0, 1), (1, 0)])]
  transfers between devices with their start and end apart: 4 -> 4, of which waited for: 4 -> 4; matrix products, arithmetic and copies ran while one was open for 7% -> 5% of each run, Pallas kernels for 0% -> 0%
where the time goes in v1:
time: 162 us
  waiting for transfers between devices  118 us (73%)
  between operations  14.5 us (9%)
  blocking collectives  9.87 us (6%)
  matrix products  8.16 us (5%)
  other arithmetic  8.14 us (5%)
  starting transfers between devices  3.15 us (2%)
    reduce_scatter x1, waiting for transfers between devices, body(): cap_grad = lax.psum_scatter(cap_part, 'dp', scatter_dimension=0, tiled=True)  62.4 us
    all_gather x1, waiting for transfers between devices, body(): gathered = lax.all_gather(captions, 'dp', axis=0, tiled=True)  30.8 us
    psum x1, waiting for transfers between devices, body(): vid_grad = lax.psum(vid_part, 'tensor')  19.9 us
    pmax x1, blocking collectives, body(): row_max = lax.pmax(stats[0], 'tensor')  4.93 us
    psum x1, blocking collectives, body(): lax.psum((stats[1] * jnp.exp(stats[0] - row_max), stats[2]), 'tensor')  4.93 us
    ppermute x1, waiting for transfers between devices, body(): lax.ppermute(partial_value, 'tensor', [(0, 1), (1, 0)])  4.87 us
  transfers between devices with their start and end apart: 4, of which 4 were waited for; matrix products, arithmetic and copies ran while one was open for 5% of the time, Pallas kernels for 0%

profile of v1, /device:TPU:0, one launch (start us, length us, event | category | flops | bytes accessed | tf_op | source)
XLA Modules:
  0.0 161.8 jit_solution(6086353623730253822)
XLA Ops:
  7.2 0.0 copy-start
  7.2 0.0 all-gather.2.cloned.1.call-start
  7.2 1.0 fusion.6
  8.3 1.6 fusion.2
  9.8 0.0 all-gather.2.cloned.1.call-update
  9.8 0.0 all-reduce.3.cloned.1.call-start
  9.9 0.0 copy-done
  9.9 1.2 fusion.12
  11.1 3.0 %collective-permute-start = (f32[128,512]{1,0:T(8,128)S(1)}, f32[128,512]{1,0:T(8,128)S(1)}, u32[]{:S(2)}, u32[]{:S(2)}) collective-permute-start(f32[128,512]{1,0:T(8,128)S(1)} %fusion.12), channel_id=1, source_target_pairs={{0,1},{1,0},{2,3},{3,2},{4,5},{5,4},{6,7},{7,6},{8,9},{9,8},{10,11... | collective-permute-start | bytes 786440 | tf_op jit(solution)/shard_map/ppermute | solution.py:43
  14.8 0.8 compare_select_fusion
  15.5 4.9 %collective-permute-done = f32[128,512]{1,0:T(8,128)S(1)} collective-permute-done((f32[128,512]{1,0:T(8,128)S(1)}, f32[128,512]{1,0:T(8,128)S(1)}, u32[]{:S(2)}, u32[]{:S(2)}) %collective-permute-start) | collective-permute-done | bytes 262176 | tf_op jit(solution)/shard_map/ppermute | solution.py:43
  20.4 0.1 multiply_reduce_fusion.1
  20.5 30.8 %all-gather.2.cloned.1.call-done = bf16[1024,512]{1,0:T(8,128)(2,1)} async-done(((bf16[64,512]{1,0:T(8,128)(2,1)}), bf16[1024,512]{1,0:T(8,128)(2,1)}) %all-gather.2.cloned.1.call-update) | async-done | bytes 1048592 | tf_op jit(solution)/shard_map/all_gather | solution.py:61
  51.3 0.0 copy-start.2
  51.3 1.9 %fusion.11 = (f32[128]{0:T(128)S(1)}, f32[128,1024]{1,0:T(8,128)S(1)}) fusion(bf16[1024,512]{1,0:T(8,128)(2,1)} %all-gather.2.cloned.1.call-done, f32[128,512]{1,0:T(8,128)S(1)} %get-tuple-element.8, f32[128]{0:T(128)S(1)} %add_rsqrt_fusion.1, f32[]{:T(128)} %bitcast.7), kind=kOutput, calls=%fused_computation.40 | convolution fusion | flops 134610816 | bytes 1836036 | tf_op jit(solution)/shard_map/dot_general | solution.py:16
  53.2 4.9 %pmax.7 = f32[128]{0:T(128)S(1)} all-reduce(f32[128]{0:T(128)S(1)} %broadcast_maximum_fusion), channel_id=1, replica_groups=mesh['dp'=16,'tensor'=2] {'tensor'}, use_global_device_ids=true, to_apply=%region_3.4 | all-reduce | flops 128 | bytes 1024 | tf_op jit(solution)/shard_map/pmax | solution.py:63
  58.1 0.3 select_reduce_fusion
  58.4 4.9 %all-reduce = (f32[128]{0:T(128)S(1)}, f32[128]{0:T(128)S(1)}) all-reduce(f32[128]{0:T(128)S(1)} %exponential_multiply_fusion, f32[128]{0:T(128)S(1)} %get-tuple-element.3), channel_id=1, replica_groups=mesh['dp'=16,'tensor'=2] {'tensor'}, use_global_device_ids=true, to_apply=%region_5.6 | all-reduce | flops 256 | bytes 2048 | tf_op jit(solution)/shard_map/psum | solution.py:64
  63.4 0.0 copy-done.2
  63.4 1.1 convolution_multiply_fusion.2
  64.5 0.0 all-reduce.3.cloned.1.call-update
  64.5 0.0 reduce-scatter.2.cloned.1.call-start
  64.5 2.0 %convolution_multiply_fusion = f32[1024,512]{1,0:T(8,128)} fusion(f32[]{:T(128)} %bitcast.8, f32[128,512]{1,0:T(8,128)S(1)} %get-tuple-element.8, f32[128]{0:T(128)S(1)} %add_rsqrt_fusion.1, f32[128,1024]{1,0:T(8,128)S(1)} %get-tuple-element.10, s32[128]{0:T(128)S(1)} %compare_select_fusion, f32[128]{0:T(128)S(1)} %get-tuple-element.5, f32[128]{0:T(128)S(1)} %pmax.7), kind=kOutput, calls=%fused_computation | convolution fusion | flops 135659520 | bytes 2885636 | tf_op jit(solution)/shard_map/dot_general | solution.py:68
  66.5 0.0 copy-start.1
  66.5 0.0 reduce-scatter.2.cloned.1.call-update
  66.5 0.5 add_subtract_fusion
  67.0 19.9 %all-reduce.3.cloned.1.call-done = f32[128,512]{1,0:T(8,128)} async-done(((f32[128,512]{1,0:T(8,128)}), f32[128,512]{1,0:T(8,128)}) %all-reduce.3.cloned.1.call-update) | async-done | bytes 262160 | tf_op jit(solution)/shard_map/psum | solution.py:67
  86.9 1.1 multiply_reduce_fusion
  88.0 2.0 %fusion.7 = f32[128,640]{1,0:T(8,128)} fusion(bf16[640,512]{1,0:T(8,128)(2,1)S(1)} %copy-done, f32[128,512]{1,0:T(8,128)} %all-reduce.3.cloned.1.call-done, f32[128,512]{1,0:T(8,128)S(1)} %get-tuple-element.8, f32[128]{0:T(128)S(1)} %multiply_reduce_fusion, f32[128]{0:T(128)S(1)} %add_rsqrt_fusion.1), kind=kOutput, calls=%fused_computation.20 | convolution fusion | flops 84213760 | bytes 1508352 | tf_op jit(solution)/shard_map/dot_general | solution.py:74
  90.1 62.4 %reduce-scatter.2.cloned.1.call-done = f32[64,512]{1,0:T(8,128)} async-done(((f32[1024,512]{1,0:T(8,128)}), f32[64,512]{1,0:T(8,128)}) %reduce-scatter.2.cloned.1.call-update) | async-done | bytes 131088 | tf_op jit(solution)/shard_map/reduce_scatter | solution.py:71
  152.5 0.0 copy-done.1
  152.5 1.1 fusion.3
  153.6 1.7 %fusion.5 = f32[64,512]{1,0:T(8,128)} fusion(f32[64,512]{1,0:T(8,128)} %reduce-scatter.2.cloned.1.call-done, bf16[64,512]{1,0:T(8,128)(2,1)S(1)} %copy-done.1, f32[64]{0:T(128)S(1)} %fusion.3, f32[64]{0:T(128)S(1)} %add_rsqrt_fusion), kind=kLoop, calls=%fused_computation.18 | loop fusion | flops 163840 | bytes 328192 | tf_op jit(solution)/shard_map/mul | solution.py:78
  (4 shorter events, 0.0 us)
Async XLA Ops:
  7.2 2.7 %copy-start = (bf16[640,512]{1,0:T(8,128)(2,1)S(1)}, bf16[640,512]{1,0:T(8,128)(2,1)}, u32[]{:S(2)}) copy-start(bf16[640,512]{1,0:T(8,128)(2,1)} %param.6) | copy-start | bytes 1966084
  7.2 44.1 %all-gather.2.cloned.1.call-start = ((), (), s32[]{:S(2)}) async-start(), calls=%async_computation.1 | async-start | bytes 1114112 | tf_op jit(solution)/shard_map/all_gather | solution.py:61
  9.8 77.1 %all-reduce.3.cloned.1.call-start = ((), (), s32[]{:S(2)}) async-start(), calls=%async_computation.2 | async-start | bytes 524288 | tf_op jit(solution)/shard_map/psum | solution.py:67
  11.1 9.3 %collective-permute-start = (f32[128,512]{1,0:T(8,128)S(1)}, f32[128,512]{1,0:T(8,128)S(1)}, u32[]{:S(2)}, u32[]{:S(2)}) collective-permute-start(f32[128,512]{1,0:T(8,128)S(1)} %fusion.12), channel_id=1, source_target_pairs={{0,1},{1,0},{2,3},{3,2},{4,5},{5,4},{6,7},{7,6},{8,9},{9,8},{10,11... | collective-permute-start | bytes 786440 | tf_op jit(solution)/shard_map/ppermute | solution.py:43
  51.3 12.0 %copy-start.2 = (bf16[1024,512]{1,0:T(8,128)(2,1)S(1)}, bf16[1024,512]{1,0:T(8,128)(2,1)}, u32[]{:S(2)}) copy-start(bf16[1024,512]{1,0:T(8,128)(2,1)} %all-gather.2.cloned.1.call-done) | copy-start | bytes 3145732
  64.5 88.0 %reduce-scatter.2.cloned.1.call-start = ((), (), s32[]{:S(2)}) async-start(), calls=%async_computation.3 | async-start | bytes 2228224 | tf_op jit(solution)/shard_map/reduce_scatter | solution.py:71
  66.5 86.0 %copy-start.1 = (bf16[64,512]{1,0:T(8,128)(2,1)S(1)}, bf16[64,512]{1,0:T(8,128)(2,1)}, u32[]{:S(2)}) copy-start(bf16[64,512]{1,0:T(8,128)(2,1)} %param.7) | copy-start | bytes 196612
Sparse Core Ops, SparseCore 0:
  10.7 40.5 all-gather.1
  64.6 22.2 all-reduce.2
  90.7 61.8 reduce-scatter.1
